TPU v7x, 32 devices: a whole 2x2x4 slice. The times are simulated.
32 devices in a mesh: rows: 4 (over z), cent: 8 (over y, x, core).
Axes of the slice: x: 2, y: 2, z: 4, core: 2. Of those that a mesh axis runs over, the one named last changes fastest.
Arguments:
- train_rows: float32 [16384, 64], P('rows'), may hold values from -6 to 6
- centre_index: int32 [16384], P('cent'), may hold values from 0 to 16383
- precond: bfloat16 [16384, 16384], P('cent', 'rows'), as said below
- coefficients: float32 [16384, 128], P(('rows', 'cent')), may hold values from -6 to 6
- residual: float32 [16384, 128], P(('rows', 'cent')), may hold values from -6 to 6
- direction: float32 [16384, 128], P(('rows', 'cent')), may hold values from -6 to 6
Outputs:
- coef_next: float32 [16384, 128], P(('rows', 'cent'))
- residual_next: float32 [16384, 128], P(('rows', 'cent'))
- direction_next: float32 [16384, 128], P(('rows', 'cent'))
Inputs may be any that keep to these rules, and one draw needn't show every extreme that they name: precond is zero below its diagonal.
All inputs are finite; a program needn't handle non-finite values.
Results may differ from a plain program's by a relative error of at most 0.0047.
Values may be sent and summed in bfloat16 or wider, within the bound.
A program may use at most 128 MiB of HBM per device.

v0:
```python
import math
import jax
import jax.numpy as jnp
from jax import lax
from jax.sharding import PartitionSpec as P

FEAT = 64
OUTS = 128
ridge_weight = 0.1


def kernel_tile(block_rows, centres):
    row_sq = jnp.sum(block_rows * block_rows, axis=1)
    cen_sq = jnp.sum(centres * centres, axis=1)
    cross = jnp.dot(
        block_rows, centres.T, precision=lax.Precision.HIGHEST, preferred_element_type=jnp.float32
    )
    distance = row_sq[:, None] + cen_sq[None, :] - 2.0 * cross
    return jnp.exp(-(2.0 / FEAT) * distance).astype(jnp.bfloat16)


def kernel_pass(local_rows, centres, coef_field, combine):
    count_rows = local_rows.shape[0]
    block_size = math.gcd(count_rows, 1024)
    block_count = count_rows // block_size
    groups = local_rows.reshape(block_count, block_size, FEAT)
    tiles = lax.map(lambda group_rows: kernel_tile(group_rows, centres), groups)
    fitted_part = jnp.einsum(
        "kbc,cd->kbd", tiles, coef_field, preferred_element_type=jnp.float32
    ).reshape(count_rows, OUTS)
    fitted = combine(fitted_part)
    fitted_groups = fitted.reshape(block_count, block_size, OUTS)
    grad_part = jnp.einsum("kbc,kbd->cd", tiles, fitted_groups, preferred_element_type=jnp.float32)
    return grad_part


def on_device(train_rows, centre_index, precond, coefficients, residual, direction):
    rows_here = train_rows.shape[0]
    start_row = lax.axis_index("rows") * rows_here
    offset = centre_index - start_row
    inside = ((offset >= 0) & (offset < rows_here)).astype(jnp.float32)
    picked = train_rows[jnp.clip(offset, 0, rows_here - 1)] * inside[:, None]
    centres = lax.psum(picked, "rows")
    dir_low = direction.astype(jnp.bfloat16)
    columns = precond
    partial_field = jnp.dot(
        columns,
        lax.all_gather(dir_low, "cent", axis=0, tiled=True),
        preferred_element_type=jnp.float32,
    )
    coef_field = lax.psum(partial_field, "rows").astype(jnp.bfloat16)

    def line_sum(part):
        return lax.psum(part, "cent").astype(jnp.bfloat16)

    grad_part = kernel_pass(train_rows, centres, coef_field, line_sum)
    grad = lax.psum(grad_part, "rows")
    grad_low = (grad * float(rows_here * lax.axis_size("rows")) ** (-0.5)).astype(jnp.bfloat16)
    columns = precond
    image = lax.psum_scatter(
        lax.dot_general(
            columns, grad_low, (((0,), (0,)), ((), ())), preferred_element_type=jnp.float32
        ),
        "cent",
        scatter_dimension=0,
        tiled=True,
    )
    image = image + ridge_weight * direction
    norm_old, curvature = lax.psum(
        (jnp.sum(residual * residual), jnp.sum(direction * image)), ("rows", "cent")
    )
    step_size = norm_old / curvature
    coef_next = coefficients + step_size * direction
    residual_next = residual - step_size * image
    norm_new = lax.psum(jnp.sum(residual_next * residual_next), ("rows", "cent"))
    direction_next = residual_next + norm_new / norm_old * direction
    return (coef_next, residual_next, direction_next)


def solution(mesh):
    placed = (
        P("rows", None),
        P("cent"),
        P("cent", "rows"),
        P(("rows", "cent"), None),
        P(("rows", "cent"), None),
        P(("rows", "cent"), None),
    )
    return jax.shard_map(
        on_device,
        mesh=mesh,
        in_specs=placed,
        out_specs=(P(("rows", "cent"), None), P(("rows", "cent"), None), P(("rows", "cent"), None)),
        check_vma=False,
    )
```

profile of v0, /device:TPU:0, one launch (start us, length us, event | category | flops | bytes accessed | tf_op | source)
XLA Modules:
  0.0 441.2 jit_solution(3471181950002680406)
XLA Ops:
  8.0 0.7 fusion.8
  8.8 0.7 and_convert_fusion
  9.5 1.8 copy.9
  11.3 5.5 %gather_fusion = f32[2048,64]{1,0:T(8,128)S(1)} fusion(f32[4096,64]{1,0:T(8,128)S(1)} %copy.9, s32[2048]{0:T(1024)S(1)} %fusion.8), kind=kCustom, calls=%fused_computation | custom fusion | bytes 1056768 | tf_op jit(solution)/shard_map/gather | solution.py:42
  16.8 1.3 broadcast_multiply_fusion
  18.2 1.6 convert_element_type.21
  19.9 53.0 %all-reduce.6.cloned.1.call-done = f32[2048,64]{1,0:T(8,128)} async-done(((f32[2048,64]{1,0:T(8,128)}), f32[2048,64]{1,0:T(8,128)}) %all-reduce.6.cloned.1.call-update) | async-done | bytes 524304 | tf_op jit(solution)/shard_map/psum | solution.py:43
  72.9 1.6 multiply_reduce_fusion
  74.5 45.0 %while.12 = (s32[]{:T(128)}, bf16[4,1024,2048]{2,1,0:T(8,128)(2,1)}, f32[4,1024,64]{2,1,0:T(8,128)S(1)}, f32[2048]{0:T(1024)S(1)}, f32[2048,64]{1,0:T(8,128)}, /*index=5*/s32[]{:T(128)}) while((s32[]{:T(128)}, bf16[4,1024,2048]{2,1,0:T(8,128)(2,1)}, f32[4,1024,64]{2,1,0:T(8,128)S(1)}, f32[2048]{0:T(1024)S(1)}, f32[2048,64]{1,0:T(8,128)}, ...), condition=%wide.region_6.7_spmd, body=%wide.region_4.0_spmd.sunk | while | flops 1621228544 | bytes 6046793 | solution.py:27
  74.5 0.2 fusion.23
  74.7 11.0 %bitcast_dynamic-update-slice_fusion.2 = bf16[4,1024,2048]{2,1,0:T(8,128)(2,1)} fusion(bf16[4,1024,2048]{2,1,0:T(8,128)(2,1)} %get-tuple-element.116, s32[]{:T(128)} %get-tuple-element.115, f32[2048,64]{1,0:T(8,128)} %get-tuple-element.125, f32[2048]{0:T(1024)S(1)} %get-tuple-element.124, f32[1024]{0:T(1024)S(1)} %fusion.23, ...), kind=kOutput, calls=%fused_computation.2.clone.1 | convolution fusion | flops 1621098496 | bytes 5780480 | tf_op jit(solution)/shard_map/while/body/eval_jaxpr/dot_general | solution.py:15
  85.7 0.2 fusion.23
  85.9 11.1 %bitcast_dynamic-update-slice_fusion.2 = bf16[4,1024,2048]{2,1,0:T(8,128)(2,1)} fusion(bf16[4,1024,2048]{2,1,0:T(8,128)(2,1)} %get-tuple-element.116, s32[]{:T(128)} %get-tuple-element.115, f32[2048,64]{1,0:T(8,128)} %get-tuple-element.125, f32[2048]{0:T(1024)S(1)} %get-tuple-element.124, f32[1024]{0:T(1024)S(1)} %fusion.23, ...), kind=kOutput, calls=%fused_computation.2.clone.1 | convolution fusion | flops 1621098496 | bytes 5780480 | tf_op jit(solution)/shard_map/while/body/eval_jaxpr/dot_general | solution.py:15
  97.0 0.2 fusion.23
  97.2 11.0 %bitcast_dynamic-update-slice_fusion.2 = bf16[4,1024,2048]{2,1,0:T(8,128)(2,1)} fusion(bf16[4,1024,2048]{2,1,0:T(8,128)(2,1)} %get-tuple-element.116, s32[]{:T(128)} %get-tuple-element.115, f32[2048,64]{1,0:T(8,128)} %get-tuple-element.125, f32[2048]{0:T(1024)S(1)} %get-tuple-element.124, f32[1024]{0:T(1024)S(1)} %fusion.23, ...), kind=kOutput, calls=%fused_computation.2.clone.1 | convolution fusion | flops 1621098496 | bytes 5780480 | tf_op jit(solution)/shard_map/while/body/eval_jaxpr/dot_general | solution.py:15
  108.4 11.1 %bitcast_dynamic-update-slice_fusion.2 = bf16[4,1024,2048]{2,1,0:T(8,128)(2,1)} fusion(bf16[4,1024,2048]{2,1,0:T(8,128)(2,1)} %get-tuple-element.116, s32[]{:T(128)} %get-tuple-element.115, f32[2048,64]{1,0:T(8,128)} %get-tuple-element.125, f32[2048]{0:T(1024)S(1)} %get-tuple-element.124, f32[1024]{0:T(1024)S(1)} %fusion.23, ...), kind=kOutput, calls=%fused_computation.2.clone.1 | convolution fusion | flops 1621098496 | bytes 5780480 | tf_op jit(solution)/shard_map/while/body/eval_jaxpr/dot_general | solution.py:15
  119.5 8.4 %fusion.10 = f32[2048,128]{1,0:T(8,128)S(1)} fusion(bf16[2048,4096]{1,0:T(8,128)(2,1)} %param.10, bf16[4096,128]{1,0:T(8,128)(2,1)} %all-gather.2.cloned.1.call-done), kind=kOutput, calls=%fused_computation.28 | convolution fusion | flops 2147483648 | bytes 18874368 | tf_op jit(solution)/shard_map/dot_general | solution.py:46
  127.9 41.5 %all-reduce.9 = bf16[2048,128]{1,0:T(8,128)(2,1)S(1)} all-reduce(f32[2048,128]{1,0:T(8,128)S(1)} %fusion.10), channel_id=1, replica_groups=mesh['rows'=4,'cent'=8] {'rows'}, use_global_device_ids=true, to_apply=%region_7.8 | all-reduce | flops 262144 | bytes 1572864 | tf_op jit(solution)/shard_map/psum | solution.py:51
  169.5 8.2 %fusion.4 = f32[4,1024,128]{2,1,0:T(8,128)S(1)} fusion(bf16[4,1024,2048]{2,1,0:T(8,128)(2,1)} %get-tuple-element.58, bf16[2048,128]{1,0:T(8,128)(2,1)S(1)} %all-reduce.9), kind=kOutput, calls=%fused_computation.12 | convolution fusion | flops 2147483648 | bytes 19398656 | tf_op jit(solution)/shard_map/kbc,cd->kbd/dot_general | solution.py:28
  177.6 56.6 %all-reduce.10 = bf16[4096,128]{1,0:T(8,128)(2,1)S(1)} all-reduce(f32[4096,128]{1,0:T(8,128)S(1)} %bitcast.34), channel_id=1, replica_groups=mesh['rows'=4,'cent'=8] {'cent'}, use_global_device_ids=true, to_apply=%region_8.9 | all-reduce | flops 524288 | bytes 3145728 | tf_op jit(solution)/shard_map/psum | solution.py:54
  234.2 9.2 %convolution_bitcast_fusion.1 = f32[2048,128]{1,0:T(8,128)} fusion(bf16[4,1024,2048]{2,1,0:T(8,128)(2,1)} %get-tuple-element.58, bf16[4,1024,128]{2,1,0:T(8,128)(2,1)S(1)} %bitcast.35), kind=kOutput, calls=%fused_computation.9 | convolution fusion | flops 2147483648 | bytes 18874368 | tf_op jit(solution)/shard_map/kbc,kbd->cd/dot_general | solution.py:33
  243.5 50.6 %all-reduce.8.cloned.1.call-done = f32[2048,128]{1,0:T(8,128)} async-done(((f32[2048,128]{1,0:T(8,128)}), f32[2048,128]{1,0:T(8,128)}) %all-reduce.8.cloned.1.call-update) | async-done | bytes 1048592 | tf_op jit(solution)/shard_map/psum | solution.py:57
  294.0 9.8 %convolution_bitcast_fusion = f32[4096,128]{0,1:T(8,128)} fusion(bf16[2048,4096]{1,0:T(8,128)(2,1)} %param.10, f32[2048,128]{1,0:T(8,128)} %all-reduce.8.cloned.1.call-done), kind=kOutput, calls=%fused_computation.8 | convolution fusion | flops 2148007936 | bytes 19922944 | tf_op jit(solution)/shard_map/dot_general | solution.py:61
  304.2 0.7 multiply_reduce_fusion.3
  304.8 39.4 %reduce-scatter.2.cloned.1.call-done = f32[512,128]{0,1:T(8,128)} async-done(((f32[4096,128]{0,1:T(8,128)}), f32[512,128]{0,1:T(8,128)}) %reduce-scatter.2.cloned.1.call-update) | async-done | bytes 262160 | tf_op jit(solution)/shard_map/reduce_scatter | solution.py:60
  344.2 1.6 multiply_reduce_fusion.2
  346.0 39.6 %all-reduce = (f32[]{:T(128)}, f32[]{:T(128)}) all-reduce(f32[]{:T(128)} %multiply_reduce_fusion.3, f32[]{:T(128)} %multiply_reduce_fusion.2), channel_id=1, replica_groups=mesh['rows'=4,'cent'=8] {'rows','cent'}, use_global_device_ids=true, to_apply=%region_1.2 | all-reduce | flops 2 | bytes 16 | tf_op jit(solution)/shard_map/psum | solution.py:69
  386.9 1.6 multiply_reduce_fusion.1
  388.6 41.3 %psum.55 = f32[]{:T(128)} all-reduce(f32[]{:T(128)} %get-tuple-element.74), channel_id=1, replica_groups=mesh['rows'=4,'cent'=8] {'rows','cent'}, use_global_device_ids=true, to_apply=%region_14.15 | all-reduce | flops 1 | bytes 8 | tf_op jit(solution)/shard_map/psum | solution.py:75
  431.2 0.8 copy.18
  432.1 0.8 copy.17
  433.0 0.8 copy.19
  (21 shorter events, 0.9 us)
Async XLA Ops:
  8.0 64.9 %all-reduce.6.cloned.1.call-start = ((), (), s32[]{:S(2)}) async-start(), calls=%async_computation.1 | async-start | bytes 2097152 | tf_op jit(solution)/shard_map/psum | solution.py:43
  18.1 101.4 %all-gather.2.cloned.1.call-start = ((), (), s32[]{:S(2)}) async-start(), calls=%async_computation.2 | async-start | bytes 1179648 | tf_op jit(solution)/shard_map/all_gather | solution.py:48
  19.8 274.2 %all-reduce.8.cloned.1.call-start = ((), (), s32[]{:S(2)}) async-start(), calls=%async_computation.3 | async-start | bytes 2097152 | tf_op jit(solution)/shard_map/psum | solution.py:57
  243.4 60.5 %copy-start = (f32[512,128]{1,0:T(8,128)S(1)}, f32[512,128]{1,0:T(8,128)}, u32[]{:S(2)}) copy-start(f32[512,128]{1,0:T(8,128)} %param.13) | copy-start | bytes 786436
  243.4 60.7 %copy-start.1 = (f32[512,128]{1,0:T(8,128)S(1)}, f32[512,128]{1,0:T(8,128)}, u32[]{:S(2)}) copy-start(f32[512,128]{1,0:T(8,128)} %param.12) | copy-start | bytes 786436
  243.4 102.5 %copy-start.2 = (f32[512,128]{1,0:T(8,128)S(1)}, f32[512,128]{1,0:T(8,128)}, u32[]{:S(2)}) copy-start(f32[512,128]{1,0:T(8,128)} %param.11) | copy-start | bytes 786436
  243.4 100.8 %reduce-scatter.2.cloned.1.call-start = ((), (), s32[]{:S(2)}) async-start(), calls=%async_computation.4 | async-start | bytes 2359296 | tf_op jit(solution)/shard_map/reduce_scatter | solution.py:60
Sparse Core Ops, SparseCore 0:
  18.2 54.6 all-reduce.5
  243.5 50.4 all-reduce.7
Sparse Core Ops, SparseCore 1:
  21.1 25.9 all-gather.1
  304.0 40.2 reduce-scatter.1
where the time goes:
time: 442 us; the launch traced here: 441 us
  blocking collectives  179 us (40%)
  waiting for transfers between devices  143 us (32%)
  matrix products  79.7 us (18%)
  between operations  18.3 us (4%)
  other arithmetic  10.7 us (2%)
  local copies, waits for them, and re-layouts  10.2 us (2%)
    psum x1, blocking collectives, line_sum(): return lax.psum(part, 'cent').astype(jnp.bfloat16)  56.6 us
    psum x1, waiting for transfers between devices, on_device(): centres = lax.psum(picked, 'rows')  53 us
    psum x1, waiting for transfers between devices, on_device(): grad = lax.psum(grad_part, 'rows')  50.6 us
    dot_general x4, matrix products, kernel_tile(): jnp.dot(block_rows, centres.T, precision=lax.Precision.HIGHEST, preferred...  44.2 us
    psum x1, blocking collectives, on_device(): coef_field = lax.psum(partial_field, 'rows').astype(jnp.bfloat16)  41.5 us
    psum x1, blocking collectives, on_device(): lax.psum(jnp.sum(residual_next * residual_next), ('rows', 'cent'))  41.3 us
    psum x1, blocking collectives, on_device(): lax.psum((jnp.sum(residual * residual), jnp.sum(direction * image)), ('ro...  39.6 us
    reduce_scatter x1, waiting for transfers between devices, on_device(): lax.psum_scatter(lax.dot_general(columns, grad_low, (((0,), (0,)), ((), (...  39.4 us
  transfers between devices with their start and end apart: 4, of which 3 were waited for; matrix products, arithmetic and copies ran while one was open for 11% of the time, Pallas kernels for 0%

commit v1 on v0

--- a/solution.py
+++ b/solution.py
@@ -54,7 +54,10 @@
         return lax.psum(part, "cent").astype(jnp.bfloat16)
 
     grad_part = kernel_pass(train_rows, centres, coef_field, line_sum)
-    grad = lax.psum(grad_part, "rows")
+    grad = grad_part
+    cores_n = lax.axis_size("rows")
+    for dd in [[(no, no ^ d) for no in range(cores_n)] for d in (1, 2, 4, 8, 16) if d < cores_n]:
+        grad = grad + lax.ppermute(grad, axis_name="rows", perm=dd)
     grad_low = (grad * float(rows_here * lax.axis_size("rows")) ** (-0.5)).astype(jnp.bfloat16)
     columns = precond
     image = lax.psum_scatter(

time: 442 us -> 461 us (1.043)
  waiting for transfers between devices: 143 us -> 160 us
    ppermute x0 -> x2, waiting for transfers between devices: none -> 65.5 us  [on_device(): grad = grad + lax.ppermute(grad, axis_name='rows', perm=dd)]
    psum x1 -> x0, waiting for transfers between devices: 50.6 us -> none  [on_device(): grad = lax.psum(grad_part, 'rows')]
  transfers between devices with their start and end apart: 4 -> 5, of which waited for: 3 -> 4; matrix products, arithmetic and copies ran while one was open for 11% -> 11% of each run, Pallas kernels for 0% -> 0%
where the time goes in v1:
time: 461 us; the launch traced here: 460 us
  blocking collectives  179 us (39%)
  waiting for transfers between devices  160 us (35%)
  matrix products  78.5 us (17%)
  between operations  18.3 us (4%)
  other arithmetic  10.8 us (2%)
  local copies, waits for them, and re-layouts  10.2 us (2%)
    ppermute x2, waiting for transfers between devices, on_device(): grad = grad + lax.ppermute(grad, axis_name='rows', perm=dd)  65.5 us
    psum x1, blocking collectives, line_sum(): return lax.psum(part, 'cent').astype(jnp.bfloat16)  56.6 us
    psum x1, waiting for transfers between devices, on_device(): centres = lax.psum(picked, 'rows')  53 us
    dot_general x4, matrix products, kernel_tile(): jnp.dot(block_rows, centres.T, precision=lax.Precision.HIGHEST, preferred...  44.2 us
    reduce_scatter x1, waiting for transfers between devices, on_device(): lax.psum_scatter(lax.dot_general(columns, grad_low, (((0,), (0,)), ((), (...  41.7 us
    psum x1, blocking collectives, on_device(): coef_field = lax.psum(partial_field, 'rows').astype(jnp.bfloat16)  41.5 us
    psum x1, blocking collectives, on_device(): lax.psum(jnp.sum(residual_next * residual_next), ('rows', 'cent'))  41.3 us
    psum x1, blocking collectives, on_device(): lax.psum((jnp.sum(residual * residual), jnp.sum(direction * image)), ('ro...  39.6 us
  transfers between devices with their start and end apart: 5, of which 4 were waited for; matrix products, arithmetic and copies ran while one was open for 11% of the time, Pallas kernels for 0%

profile of v1, /device:TPU:0, one launch (start us, length us, event | category | flops | bytes accessed | tf_op | source)
XLA Modules:
  0.0 460.3 jit_solution(7665831548889880813)
XLA Ops:
  8.0 0.7 fusion.8
  8.8 0.7 and_convert_fusion
  9.5 1.8 copy.9
  11.3 5.5 %gather_fusion = f32[2048,64]{1,0:T(8,128)S(1)} fusion(f32[4096,64]{1,0:T(8,128)S(1)} %copy.9, s32[2048]{0:T(1024)S(1)} %fusion.8), kind=kCustom, calls=%fused_computation | custom fusion | bytes 1056768 | tf_op jit(solution)/shard_map/gather | solution.py:42
  16.8 1.3 broadcast_multiply_fusion
  18.2 1.6 convert_element_type.21
  19.9 53.0 %all-reduce.5.cloned.1.call-done = f32[2048,64]{1,0:T(8,128)} async-done(((f32[2048,64]{1,0:T(8,128)}), f32[2048,64]{1,0:T(8,128)}) %all-reduce.5.cloned.1.call-update) | async-done | bytes 524304 | tf_op jit(solution)/shard_map/psum | solution.py:43
  72.9 1.6 multiply_reduce_fusion
  74.5 45.0 %while.12 = (s32[]{:T(128)}, bf16[4,1024,2048]{2,1,0:T(8,128)(2,1)}, f32[4,1024,64]{2,1,0:T(8,128)S(1)}, f32[2048]{0:T(1024)S(1)}, f32[2048,64]{1,0:T(8,128)}, /*index=5*/s32[]{:T(128)}) while((s32[]{:T(128)}, bf16[4,1024,2048]{2,1,0:T(8,128)(2,1)}, f32[4,1024,64]{2,1,0:T(8,128)S(1)}, f32[2048]{0:T(1024)S(1)}, f32[2048,64]{1,0:T(8,128)}, ...), condition=%wide.region_6.7_spmd, body=%wide.region_4.0_spmd.sunk | while | flops 1621228544 | bytes 6046793 | solution.py:27
  74.5 0.2 fusion.23
  74.7 11.0 %bitcast_dynamic-update-slice_fusion.2 = bf16[4,1024,2048]{2,1,0:T(8,128)(2,1)} fusion(bf16[4,1024,2048]{2,1,0:T(8,128)(2,1)} %get-tuple-element.116, s32[]{:T(128)} %get-tuple-element.115, f32[2048,64]{1,0:T(8,128)} %get-tuple-element.125, f32[2048]{0:T(1024)S(1)} %get-tuple-element.124, f32[1024]{0:T(1024)S(1)} %fusion.23, ...), kind=kOutput, calls=%fused_computation.2.clone.1 | convolution fusion | flops 1621098496 | bytes 5780480 | tf_op jit(solution)/shard_map/while/body/eval_jaxpr/dot_general | solution.py:15
  85.9 11.1 %bitcast_dynamic-update-slice_fusion.2 = bf16[4,1024,2048]{2,1,0:T(8,128)(2,1)} fusion(bf16[4,1024,2048]{2,1,0:T(8,128)(2,1)} %get-tuple-element.116, s32[]{:T(128)} %get-tuple-element.115, f32[2048,64]{1,0:T(8,128)} %get-tuple-element.125, f32[2048]{0:T(1024)S(1)} %get-tuple-element.124, f32[1024]{0:T(1024)S(1)} %fusion.23, ...), kind=kOutput, calls=%fused_computation.2.clone.1 | convolution fusion | flops 1621098496 | bytes 5780480 | tf_op jit(solution)/shard_map/while/body/eval_jaxpr/dot_general | solution.py:15
  97.2 11.0 %bitcast_dynamic-update-slice_fusion.2 = bf16[4,1024,2048]{2,1,0:T(8,128)(2,1)} fusion(bf16[4,1024,2048]{2,1,0:T(8,128)(2,1)} %get-tuple-element.116, s32[]{:T(128)} %get-tuple-element.115, f32[2048,64]{1,0:T(8,128)} %get-tuple-element.125, f32[2048]{0:T(1024)S(1)} %get-tuple-element.124, f32[1024]{0:T(1024)S(1)} %fusion.23, ...), kind=kOutput, calls=%fused_computation.2.clone.1 | convolution fusion | flops 1621098496 | bytes 5780480 | tf_op jit(solution)/shard_map/while/body/eval_jaxpr/dot_general | solution.py:15
  108.4 11.1 %bitcast_dynamic-update-slice_fusion.2 = bf16[4,1024,2048]{2,1,0:T(8,128)(2,1)} fusion(bf16[4,1024,2048]{2,1,0:T(8,128)(2,1)} %get-tuple-element.116, s32[]{:T(128)} %get-tuple-element.115, f32[2048,64]{1,0:T(8,128)} %get-tuple-element.125, f32[2048]{0:T(1024)S(1)} %get-tuple-element.124, f32[1024]{0:T(1024)S(1)} %fusion.23, ...), kind=kOutput, calls=%fused_computation.2.clone.1 | convolution fusion | flops 1621098496 | bytes 5780480 | tf_op jit(solution)/shard_map/while/body/eval_jaxpr/dot_general | solution.py:15
  119.5 8.4 %fusion.10 = f32[2048,128]{1,0:T(8,128)S(1)} fusion(bf16[2048,4096]{1,0:T(8,128)(2,1)} %param.10, bf16[4096,128]{1,0:T(8,128)(2,1)} %all-gather.2.cloned.1.call-done), kind=kOutput, calls=%fused_computation.28 | convolution fusion | flops 2147483648 | bytes 18874368 | tf_op jit(solution)/shard_map/dot_general | solution.py:46
  127.9 41.5 %all-reduce.6 = bf16[2048,128]{1,0:T(8,128)(2,1)S(1)} all-reduce(f32[2048,128]{1,0:T(8,128)S(1)} %fusion.10), channel_id=1, replica_groups=mesh['rows'=4,'cent'=8] {'rows'}, use_global_device_ids=true, to_apply=%region_7.8 | all-reduce | flops 262144 | bytes 1572864 | tf_op jit(solution)/shard_map/psum | solution.py:51
  169.5 8.2 %fusion.4 = f32[4,1024,128]{2,1,0:T(8,128)S(1)} fusion(bf16[4,1024,2048]{2,1,0:T(8,128)(2,1)} %get-tuple-element.58, bf16[2048,128]{1,0:T(8,128)(2,1)S(1)} %all-reduce.6), kind=kOutput, calls=%fused_computation.12 | convolution fusion | flops 2147483648 | bytes 19398656 | tf_op jit(solution)/shard_map/kbc,cd->kbd/dot_general | solution.py:28
  177.6 56.6 %all-reduce.7 = bf16[4096,128]{1,0:T(8,128)(2,1)S(1)} all-reduce(f32[4096,128]{1,0:T(8,128)S(1)} %bitcast.34), channel_id=1, replica_groups=mesh['rows'=4,'cent'=8] {'cent'}, use_global_device_ids=true, to_apply=%region_8.9 | all-reduce | flops 524288 | bytes 3145728 | tf_op jit(solution)/shard_map/psum | solution.py:54
  234.3 8.1 %convolution_bitcast_fusion.1 = f32[2048,128]{1,0:T(8,128)S(1)} fusion(bf16[4,1024,2048]{2,1,0:T(8,128)(2,1)} %get-tuple-element.58, bf16[4,1024,128]{2,1,0:T(8,128)(2,1)S(1)} %bitcast.35), kind=kOutput, calls=%fused_computation.9 | convolution fusion | flops 2147483648 | bytes 18874368 | tf_op jit(solution)/shard_map/kbc,kbd->cd/dot_general | solution.py:33
  242.5 22.9 %collective-permute-done = f32[2048,128]{1,0:T(8,128)S(1)} collective-permute-done((f32[2048,128]{1,0:T(8,128)S(1)}, f32[2048,128]{1,0:T(8,128)S(1)}, u32[]{:S(2)}, u32[]{:S(2)}) %collective-permute-start) | collective-permute-done | bytes 1048608 | tf_op jit(solution)/shard_map/ppermute | solution.py:60
  265.6 2.9 collective-permute-start.1
  268.5 42.6 %collective-permute-done.1 = f32[2048,128]{1,0:T(8,128)S(1)} collective-permute-done((f32[2048,128]{1,0:T(8,128)S(1)}, f32[2048,128]{1,0:T(8,128)S(1)}, u32[]{:S(2)}, u32[]{:S(2)}) %collective-permute-start.1) | collective-permute-done | bytes 1048608 | tf_op jit(solution)/shard_map/ppermute | solution.py:60
  311.1 9.6 %convolution_bitcast_fusion = f32[4096,128]{0,1:T(8,128)} fusion(bf16[2048,4096]{1,0:T(8,128)(2,1)} %param.10, f32[2048,128]{1,0:T(8,128)S(1)} %add.57, f32[2048,128]{1,0:T(8,128)S(1)} %collective-permute-done.1), kind=kOutput, calls=%fused_computation.8 | convolution fusion | flops 2148270080 | bytes 20971520 | tf_op jit(solution)/shard_map/dot_general | solution.py:64
  321.0 0.7 multiply_reduce_fusion.3
  321.6 41.7 %reduce-scatter.2.cloned.1.call-done = f32[512,128]{0,1:T(8,128)} async-done(((f32[4096,128]{0,1:T(8,128)}), f32[512,128]{0,1:T(8,128)}) %reduce-scatter.2.cloned.1.call-update) | async-done | bytes 262160 | tf_op jit(solution)/shard_map/reduce_scatter | solution.py:63
  363.3 1.6 multiply_reduce_fusion.2
  365.1 39.6 %all-reduce = (f32[]{:T(128)}, f32[]{:T(128)}) all-reduce(f32[]{:T(128)} %multiply_reduce_fusion.3, f32[]{:T(128)} %multiply_reduce_fusion.2), channel_id=1, replica_groups=mesh['rows'=4,'cent'=8] {'rows','cent'}, use_global_device_ids=true, to_apply=%region_1.2 | all-reduce | flops 2 | bytes 16 | tf_op jit(solution)/shard_map/psum | solution.py:72
  406.0 1.6 multiply_reduce_fusion.1
  407.7 41.3 %psum.47 = f32[]{:T(128)} all-reduce(f32[]{:T(128)} %get-tuple-element.74), channel_id=1, replica_groups=mesh['rows'=4,'cent'=8] {'rows','cent'}, use_global_device_ids=true, to_apply=%region_13.14 | all-reduce | flops 1 | bytes 8 | tf_op jit(solution)/shard_map/psum | solution.py:78
  450.3 0.8 copy.19
  451.2 0.8 copy.18
  452.1 0.8 copy.20
  (23 shorter events, 1.5 us)
Async XLA Ops:
  8.0 64.9 %all-reduce.5.cloned.1.call-start = ((), (), s32[]{:S(2)}) async-start(), calls=%async_computation.1 | async-start | bytes 2097152 | tf_op jit(solution)/shard_map/psum | solution.py:43
  18.1 101.4 %all-gather.2.cloned.1.call-start = ((), (), s32[]{:S(2)}) async-start(), calls=%async_computation.2 | async-start | bytes 1179648 | tf_op jit(solution)/shard_map/all_gather | solution.py:48
  19.8 343.5 %reduce-scatter.2.cloned.1.call-start = ((), (), s32[]{:S(2)}) async-start(), calls=%async_computation.3 | async-start | bytes 2359296 | tf_op jit(solution)/shard_map/reduce_scatter | solution.py:63
  242.4 78.3 %copy-start = (f32[512,128]{1,0:T(8,128)S(1)}, f32[512,128]{1,0:T(8,128)}, u32[]{:S(2)}) copy-start(f32[512,128]{1,0:T(8,128)} %param.13) | copy-start | bytes 786436
  242.4 78.4 %copy-start.1 = (f32[512,128]{1,0:T(8,128)S(1)}, f32[512,128]{1,0:T(8,128)}, u32[]{:S(2)}) copy-start(f32[512,128]{1,0:T(8,128)} %param.12) | copy-start | bytes 786436
  242.4 23.0 %collective-permute-start = (f32[2048,128]{1,0:T(8,128)S(1)}, f32[2048,128]{1,0:T(8,128)S(1)}, u32[]{:S(2)}, u32[]{:S(2)}) collective-permute-start(f32[2048,128]{1,0:T(8,128)S(1)} %convolution_bitcast_fusion.1), channel_id=1, source_target_pairs={{0,8},{8,0},{16,24},{24,16},{1,9},{9,1},{17,25},{25,17},{2,10},{10... | collective-permute-start | bytes 3145736 | tf_op jit(solution)/shard_map/ppermute | solution.py:60
  265.5 99.4 %copy-start.2 = (f32[512,128]{1,0:T(8,128)S(1)}, f32[512,128]{1,0:T(8,128)}, u32[]{:S(2)}) copy-start(f32[512,128]{1,0:T(8,128)} %param.11) | copy-start | bytes 786436
  265.6 45.5 %collective-permute-start.1 = (f32[2048,128]{1,0:T(8,128)S(1)}, f32[2048,128]{1,0:T(8,128)S(1)}, u32[]{:S(2)}, u32[]{:S(2)}) collective-permute-start(f32[2048,128]{1,0:T(8,128)S(1)} %add.57), channel_id=1, source_target_pairs={{0,16},{8,24},{16,0},{24,8},{1,17},{9,25},{17,1},{25,9},{2,18},{10... | collective-permute-start | bytes 3145736 | tf_op jit(solution)/shard_map/ppermute | solution.py:60
Sparse Core Ops, SparseCore 0:
  18.2 54.6 all-reduce.4
Sparse Core Ops, SparseCore 1:
  21.1 25.9 all-gather.1
  320.8 42.5 reduce-scatter.1
